TPU v7x, 256 devices: a whole 4x4x8 slice. The times are simulated.
256 devices in a mesh: tmpl: 32 (over x, z_lo, core), tm: 8 (over y, z_hi).
Axes of the slice: x: 4, y: 4, z: 8 (z_hi: 2, z_lo: 4; z = z_hi * 4 + z_lo), core: 2. Of those that a mesh axis runs over, the one named last changes fastest.
Arguments:
- records: bfloat16 [1536, 4096], P('tmpl', 'tm'), may hold values from -6 to 6
- templates: bfloat16 [2, 1024, 48, 200], P(None, 'tmpl'), may hold values from -0.0625 to 0.0625
- channels: int32 [2, 1024, 48], P(None, 'tmpl'), may hold values from 0 to 1535
- moveouts: int32 [2, 1024, 48], P(None, 'tmpl'), may hold values from 0 to 55
Outputs:
- detections: float32 [2, 1024, 4096], P(None, 'tmpl', 'tm')
All inputs are finite; a program needn't handle non-finite values.
Results may differ from a plain program's by a relative error of at most 0.0043.
Values may be sent and summed in bfloat16 or wider, within the bound.
No kernel may reach another device: no remote copies, remote signals or barrier semaphores. Data moves between devices by JAX's collectives and lax.ppermute only.
A program may use at most 64 MiB of HBM per device.

v0:
```python
import math
import jax
import jax.numpy as jnp
from jax import lax
from jax.sharding import PartitionSpec as P

L = 200
LAGS = 56


def from_behind(block, axis, distance):
    devices = range(lax.axis_size(axis))
    route = [(i - distance, i) for i in devices if i - distance in devices]
    return lax.ppermute(block, axis, route)


def tables(count, freqs, width):
    sample = jnp.arange(count, dtype=jnp.int32)[:, None]
    freq = jnp.arange(freqs, dtype=jnp.int32)[None, :]
    angle = 2.0 * math.pi / width * (sample * freq % width).astype(jnp.float32)
    return jnp.concatenate([jnp.cos(angle), jnp.sin(angle)], axis=1)


def detect(waves, chans, lags, spectra, forward, inverse, weight, freq, width, freqs):
    count = waves.shape[0]
    hspec = jnp.dot(
        waves.reshape(-1, waves.shape[2]),
        forward[: waves.shape[2]],
        preferred_element_type=jnp.float32,
    )
    h_cos, h_sin = (hspec[:, :freqs], hspec[:, freqs:])
    angle = (
        2.0
        * math.pi
        / width
        * (lags.reshape(-1)[:, None] * freq[None, :] % width).astype(jnp.float32)
    )
    c_theta, s_theta = (jnp.cos(angle), jnp.sin(angle))
    picked = spectra[chans.reshape(-1)].astype(jnp.float32)
    x_cos, x_sin = (picked[:, :freqs], picked[:, freqs:])
    prod_a = h_cos * x_cos + h_sin * x_sin
    prod_b = h_sin * x_cos - h_cos * x_sin
    real_part = (prod_a * c_theta - prod_b * s_theta).reshape(count, -1, freqs).sum(axis=1)
    imag_part = (prod_a * s_theta + prod_b * c_theta).reshape(count, -1, freqs).sum(axis=1)
    joint = jnp.concatenate([real_part * weight, -imag_part * weight], axis=1)
    return lax.dot_general(
        joint, inverse, (((1,), (1,)), ((), ())), precision=lax.Precision.HIGHEST
    )


def per_device(records, templates, channels, moveouts):
    time_dev = records.shape[1]
    extra = L + LAGS - 2
    width = time_dev + extra
    freqs = width // 2 + 1
    forward = tables(width, freqs, width).astype(jnp.bfloat16)
    inverse = tables(time_dev, freqs, width)
    freq = jnp.arange(freqs, dtype=jnp.int32)
    weight = jnp.where((freq == 0) | (freq == freqs - 1), 1.0, 2.0).astype(jnp.float32) / width
    rim = from_behind(records[:, :extra], "tm", -1)
    window = jnp.concatenate([records, rim], axis=1)
    spectra = jnp.dot(
        lax.all_gather(window, "tmpl", axis=0, tiled=True),
        forward,
        preferred_element_type=jnp.float32,
    ).astype(jnp.bfloat16)
    results = []
    for batch in range(templates.shape[0]):
        results.append(
            detect(
                templates[batch],
                channels[batch],
                moveouts[batch],
                spectra,
                forward,
                inverse,
                weight,
                freq,
                width,
                freqs,
            )
        )
    return jnp.stack(results)


def solution(mesh):
    placed = (
        P("tmpl", "tm"),
        P(None, "tmpl", None, None),
        P(None, "tmpl", None),
        P(None, "tmpl", None),
    )
    return jax.shard_map(
        per_device, mesh=mesh, in_specs=placed, out_specs=P(None, "tmpl", "tm"), check_vma=False
    )
```

profile of v0, /device:TPU:1, one launch (start us, length us, event | category | flops | bytes accessed | tf_op | source)
XLA Modules:
  0.0 185.4 jit_solution(2177436032640914762)
XLA Ops:
  8.7 9.6 %collective-permute-done = bf16[48,254]{1,0:T(8,128)(2,1)S(1)} collective-permute-done((bf16[48,254]{1,0:T(8,128)(2,1)S(1)}, bf16[48,254]{1,0:T(8,128)(2,1)S(1)}, u32[]{:S(2)}, u32[]{:S(2)}) %collective-permute-start) | collective-permute-done | bytes 24416 | tf_op jit(solution)/shard_map/ppermute | solution.py:14
  21.6 5.0 %sine_convert_fusion = (bf16[766,384]{1,0:T(8,128)(2,1)S(1)}, bf16[766,384]{1,0:T(8,128)(2,1)S(1)}) fusion(), kind=kLoop, calls=%fused_computation.41 | loop fusion | flops 3235584 | bytes 1176576 | tf_op jit(solution)/shard_map/convert.1
  27.7 4.2 %fusion.30 = (f32[512,384]{1,0:T(8,128)S(1)}, f32[512,384]{1,0:T(8,128)}) fusion(), kind=kLoop, calls=%fused_computation.54 | loop fusion | flops 1769472 | bytes 1572864 | tf_op jit(solution)/shard_map/sin | solution.py:21
  32.1 3.0 %convolution_bitcast_fusion = f32[1536,768]{0,1:T(8,128)} fusion(bf16[200,768]{1,0:T(8,128)(2,1)S(1)} %pad_maximum_fusion.7, bf16[1536,200]{1,0:T(8,128)(2,1)S(1)} %bitcast.24), kind=kOutput, calls=%fused_computation.2 | convolution fusion | flops 471859200 | bytes 5640192 | tf_op jit(solution)/shard_map/dot_general | solution.py:26
  35.1 3.0 %convolution_bitcast_fusion.1 = f32[1536,768]{0,1:T(8,128)} fusion(bf16[200,768]{1,0:T(8,128)(2,1)S(1)} %pad_maximum_fusion.7, bf16[1536,200]{1,0:T(8,128)(2,1)S(1)} %bitcast.23), kind=kOutput, calls=%fused_computation.3 | convolution fusion | flops 471859200 | bytes 5640192 | tf_op jit(solution)/shard_map/dot_general | solution.py:26
  38.0 46.4 %all-gather.2.cloned.1.call-done = bf16[1536,766]{1,0:T(8,128)(2,1)} async-done(((bf16[48,766]{1,0:T(8,128)(2,1)}), bf16[1536,766]{1,0:T(8,128)(2,1)}) %all-gather.2.cloned.1.call-update) | async-done | bytes 2353168 | tf_op jit(solution)/shard_map/all_gather | solution.py:63
  84.4 4.0 %convolution_convert_fusion = bf16[1536,768]{1,0:T(8,128)(2,1)S(1)} fusion(bf16[1536,766]{1,0:T(8,128)(2,1)} %all-gather.2.cloned.1.call-done, bf16[766,384]{1,0:T(8,128)(2,1)} %copy-done.3, bf16[766,384]{1,0:T(8,128)(2,1)} %copy-done.4), kind=kOutput, calls=%fused_computation.6 | convolution fusion | flops 1810753536 | bytes 5889024 | tf_op jit(solution)/shard_map/dot_general | solution.py:62
  88.4 5.7 %gather_fusion.1 = bf16[1536,768]{1,0:T(8,128)(2,1)} fusion(bf16[1536,768]{1,0:T(8,128)(2,1)S(1)} %convolution_convert_fusion, s32[2048]{0:T(1024)S(1)} %pad_clamp_fusion), kind=kCustom, calls=%fused_computation.1 | custom fusion | bytes 4724736 | tf_op jit(solution)/shard_map/gather | solution.py:39
  94.1 4.3 %copy.10 = bf16[1536,768]{0,1:T(8,128)(2,1)} copy(bf16[1536,768]{1,0:T(8,128)(2,1)} %gather_fusion.1) | data formatting | bytes 4718592 | tf_op jit(solution)/shard_map/gather | solution.py:39
  98.3 2.3 %convert_element_type.31 = f32[1536,768]{0,1:T(8,128)S(1)} convert(bf16[1536,768]{0,1:T(8,128)(2,1)} %copy.10) | non-fusion elementwise | flops 1179648 | bytes 7077888 | tf_op jit(solution)/shard_map/convert_element_type | solution.py:39
  100.6 13.5 %multiply_subtract_fusion = (f32[1536,384]{0,1:T(8,128)}, f32[1536,384]{0,1:T(8,128)S(1)}, f32[1536,384]{0,1:T(8,128)S(1)}) fusion(s32[1536]{0:T(1024)S(1)} %mul.198, f32[1536,768]{0,1:T(8,128)S(1)} %convert_element_type.31, f32[1536,768]{0,1:T(8,128)} %convolution_bitcast_fusion), kind=kLoop, calls=%fused_computation.12 | loop fusion | flops 10616832 | bytes 16521216 | tf_op jit(solution)/shard_map/sub | solution.py:43
  114.1 10.8 %multiply_add_fusion = f32[1536,384]{0,1:T(8,128)} fusion(f32[1536,384]{0,1:T(8,128)S(1)} %get-tuple-element.10, f32[1536,384]{0,1:T(8,128)S(1)} %get-tuple-element.9, s32[1536]{0:T(1024)S(1)} %mul.198), kind=kLoop, calls=%fused_computation.11 | loop fusion | flops 7077888 | bytes 7084032 | tf_op jit(solution)/shard_map/add | solution.py:44
  124.9 3.1 %copy.12 = f32[1536,384]{1,0:T(8,128)} copy(f32[1536,384]{0,1:T(8,128)} %multiply_add_fusion) | data formatting | bytes 4718592 | tf_op jit(solution)/shard_map/add | solution.py:44
  128.1 5.7 %gather_fusion = bf16[1536,768]{1,0:T(8,128)(2,1)} fusion(bf16[1536,768]{1,0:T(8,128)(2,1)S(1)} %convolution_convert_fusion, s32[2048]{0:T(1024)S(1)} %pad_clamp_fusion.1), kind=kCustom, calls=%fused_computation | custom fusion | bytes 4724736 | tf_op jit(solution)/shard_map/gather | solution.py:39
  133.7 2.8 %copy.7 = bf16[1536,768]{0,1:T(8,128)(2,1)S(1)} copy(bf16[1536,768]{1,0:T(8,128)(2,1)} %gather_fusion) | data formatting | bytes 4718592 | tf_op jit(solution)/shard_map/gather | solution.py:39
  137.2 13.5 %multiply_subtract_fusion.2 = (f32[1536,384]{0,1:T(8,128)}, f32[1536,384]{0,1:T(8,128)S(1)}, f32[1536,384]{0,1:T(8,128)S(1)}) fusion(s32[1536]{0:T(1024)S(1)} %mul.177, f32[1536,768]{0,1:T(8,128)S(1)} %convert_element_type.28, f32[1536,768]{0,1:T(8,128)} %convolution_bitcast_fusion.1), kind=kLoop, calls=%fused_computation.21 | loop fusion | flops 10616832 | bytes 16521216 | tf_op jit(solution)/shard_map/sub | solution.py:43
  150.7 9.9 %multiply_add_fusion.2 = f32[1536,384]{0,1:T(8,128)S(1)} fusion(f32[1536,384]{0,1:T(8,128)S(1)} %get-tuple-element.7, f32[1536,384]{0,1:T(8,128)S(1)} %get-tuple-element.6, s32[1536]{0:T(1024)S(1)} %mul.177), kind=kLoop, calls=%fused_computation.20 | loop fusion | flops 7077888 | bytes 7084032 | tf_op jit(solution)/shard_map/add | solution.py:44
  160.6 2.0 %copy.9 = f32[1536,384]{1,0:T(8,128)} copy(f32[1536,384]{0,1:T(8,128)S(1)} %multiply_add_fusion.2) | data formatting | bytes 4718592 | tf_op jit(solution)/shard_map/add | solution.py:44
  162.6 2.0 %reduce_sum.39 = f32[32,384]{1,0:T(8,128)S(1)} reduce(f32[32,48,384]{2,1,0:T(8,128)} %bitcast.19, f32[]{:T(128)} %constant.26.clone.1), dimensions={1}, to_apply=%region_3.4 | reduce | flops 577536 | bytes 2408452 | tf_op jit(solution)/shard_map/reduce_sum | solution.py:44
  164.6 1.9 %reduce_sum.37 = f32[32,384]{1,0:T(8,128)S(1)} reduce(f32[32,48,384]{2,1,0:T(8,128)} %bitcast.20, f32[]{:T(128)} %constant.26.clone.1), dimensions={1}, to_apply=%region_1.2 | reduce | flops 577536 | bytes 2408452 | tf_op jit(solution)/shard_map/reduce_sum | solution.py:44
  166.5 2.0 %copy.11 = f32[1536,384]{1,0:T(8,128)} copy(f32[1536,384]{0,1:T(8,128)S(1)} %copy-done) | data formatting | bytes 4718592 | tf_op jit(solution)/shard_map/sub | solution.py:43
  168.5 2.0 %reduce_sum.38 = f32[32,384]{1,0:T(8,128)S(1)} reduce(f32[32,48,384]{2,1,0:T(8,128)} %bitcast.22, f32[]{:T(128)} %constant.26.clone.1), dimensions={1}, to_apply=%region_2.3 | reduce | flops 577536 | bytes 2408452 | tf_op jit(solution)/shard_map/reduce_sum | solution.py:43
  170.8 2.0 %copy.8 = f32[1536,384]{1,0:T(8,128)} copy(f32[1536,384]{0,1:T(8,128)S(1)} %copy-done.1) | data formatting | bytes 4718592 | tf_op jit(solution)/shard_map/sub | solution.py:43
  172.8 1.9 %reduce_sum.36 = f32[32,384]{1,0:T(8,128)S(1)} reduce(f32[32,48,384]{2,1,0:T(8,128)} %bitcast.21, f32[]{:T(128)} %constant.26.clone.1), dimensions={1}, to_apply=%region_0.1 | reduce | flops 577536 | bytes 2408452 | tf_op jit(solution)/shard_map/reduce_sum | solution.py:43
  (35 shorter events, 11.4 us)
Async XLA Ops:
  6.5 77.9 %all-gather.2.cloned.1.call-start = ((), (), s32[]{:S(2)}) async-start(), calls=%async_computation | async-start | bytes 2433024 | tf_op jit(solution)/shard_map/all_gather | solution.py:63
  7.3 24.7 %copy-start.5 = (bf16[2,32,48,200]{3,2,1,0:T(8,128)(2,1)S(1)}, bf16[2,32,48,200]{3,2,1,0:T(8,128)(2,1)}, u32[]{:S(2)}) copy-start(bf16[2,32,48,200]{3,2,1,0:T(8,128)(2,1)} %param.5) | copy-start | bytes 3686404
  7.3 11.0 %collective-permute-start = (bf16[48,254]{1,0:T(8,128)(2,1)S(1)}, bf16[48,254]{1,0:T(8,128)(2,1)S(1)}, u32[]{:S(2)}, u32[]{:S(2)}) collective-permute-start(bf16[48,254]{1,0:T(8,128)(2,1)S(1)} %slice.52), channel_id=1, source_target_pairs={{1,0},{2,1},{3,2},{4,3},{5,4},{6,5},{7,6},{9,8},{10,9},{11,10},{12... | collective-permute-start | bytes 73160 | tf_op jit(solution)/shard_map/ppermute | solution.py:14
  26.6 0.8 copy-start.3
  26.6 1.1 copy-start.4
  162.6 3.9 %copy-start = (f32[1536,384]{0,1:T(8,128)S(1)}, f32[1536,384]{0,1:T(8,128)}, u32[]{:S(2)}) copy-start(f32[1536,384]{0,1:T(8,128)} %get-tuple-element.8) | copy-start | bytes 7077892
  168.5 2.4 %copy-start.1 = (f32[1536,384]{0,1:T(8,128)S(1)}, f32[1536,384]{0,1:T(8,128)}, u32[]{:S(2)}) copy-start(f32[1536,384]{0,1:T(8,128)} %get-tuple-element.5) | copy-start | bytes 7077892
  172.8 2.0 %copy-start.2 = (f32[512,384]{1,0:T(8,128)S(1)}, f32[512,384]{1,0:T(8,128)}, u32[]{:S(2)}) copy-start(f32[512,384]{1,0:T(8,128)} %get-tuple-element.24) | copy-start | bytes 2359300
Sparse Core Ops, SparseCore 0:
  19.8 64.5 all-gather.1
where the time goes:
time: 186 us; the launch traced here: 185 us
  other arithmetic  69.9 us (38%)
  waiting for transfers between devices  56 us (30%)
  local copies, waits for them, and re-layouts  31.5 us (17%)
  between operations  13.6 us (7%)
  matrix products  13 us (7%)
    all_gather x1, waiting for transfers between devices, per_device(): lax.all_gather(window, 'tmpl', axis=0, tiled=True)  46.4 us
    sub x2, other arithmetic, detect(): prod_a * c_theta - prod_b * s_theta  27.1 us
    add x2, other arithmetic, detect(): prod_a * s_theta + prod_b * c_theta  20.6 us
    gather x4, local copies, waits for them, and re-layouts, detect(): picked = spectra[chans.reshape(-1)].astype(jnp.float32)  18.4 us
    ppermute x1, waiting for transfers between devices, from_behind(): return lax.ppermute(block, axis, route)  9.56 us
    dot_general x2, matrix products, detect(): jnp.dot(waves.reshape(-1, waves.shape[2]), forward[:waves.shape[2]], pref...  5.98 us
    add x2, local copies, waits for them, and re-layouts, detect(): prod_a * s_theta + prod_b * c_theta  5.11 us
    another operation x1, other arithmetic  5 us
  transfers between devices with their start and end apart: 2, of which 2 were waited for; matrix products, arithmetic and copies ran while one was open for 9% of the time, Pallas kernels for 0%

commit v1 on v0

--- a/solution.py
+++ b/solution.py
@@ -60,7 +60,9 @@
     rim = from_behind(records[:, :extra], "tm", -1)
     window = jnp.concatenate([records, rim], axis=1)
     spectra = jnp.dot(
-        lax.all_gather(window, "tmpl", axis=0, tiled=True),
+        jnp.concatenate(
+            lax.all_to_all(jnp.stack([window] * lax.axis_size("tmpl")), "tmpl", 0, 0), axis=0
+        ),
         forward,
         preferred_element_type=jnp.float32,
     ).astype(jnp.bfloat16)

time: 186 us -> 175 us (0.941)
  between operations: 13.6 us -> 0.24 us
  starting transfers between devices: 1.41 us -> 10.2 us
  waiting for transfers between devices: 56 us -> 47.9 us
    all_gather x1 -> x0, waiting for transfers between devices: 46.4 us -> none  [per_device(): lax.all_gather(window, 'tmpl', axis=0, tiled=True)]
    all_to_all x0 -> x1, waiting for transfers between devices: none -> 38.4 us  [per_device(): lax.all_to_all(jnp.stack([window] * lax.axis_size('tmpl')), 'tmpl', 0, 0)]
    all_to_all x0 -> x1, starting transfers between devices: none -> 8.92 us  [per_device(): lax.all_to_all(jnp.stack([window] * lax.axis_size('tmpl')), 'tmpl', 0, 0)]
where the time goes in v1:
time: 175 us; the launch traced here: 174 us
  other arithmetic  69.3 us (40%)
  waiting for transfers between devices  47.9 us (27%)
  local copies, waits for them, and re-layouts  33 us (19%)
  matrix products  13 us (7%)
  starting transfers between devices  10.2 us (6%)
    all_to_all x1, waiting for transfers between devices, per_device(): lax.all_to_all(jnp.stack([window] * lax.axis_size('tmpl')), 'tmpl', 0, 0)  38.4 us
    sub x2, other arithmetic, detect(): prod_a * c_theta - prod_b * s_theta  27.1 us
    add x2, other arithmetic, detect(): prod_a * s_theta + prod_b * c_theta  20.6 us
    gather x4, local copies, waits for them, and re-layouts, detect(): picked = spectra[chans.reshape(-1)].astype(jnp.float32)  18.4 us
    ppermute x1, waiting for transfers between devices, from_behind(): return lax.ppermute(block, axis, route)  9.56 us
    all_to_all x1, starting transfers between devices, per_device(): lax.all_to_all(jnp.stack([window] * lax.axis_size('tmpl')), 'tmpl', 0, 0)  8.92 us
    dot_general x2, matrix products, detect(): jnp.dot(waves.reshape(-1, waves.shape[2]), forward[:waves.shape[2]], pref...  5.99 us
    add x2, local copies, waits for them, and re-layouts, detect(): prod_a * s_theta + prod_b * c_theta  5.13 us
  transfers between devices with their start and end apart: 2, of which 2 were waited for; matrix products, arithmetic and copies ran while one was open for 9% of the time, Pallas kernels for 0%

profile of v1, /device:TPU:1, one launch (start us, length us, event | category | flops | bytes accessed | tf_op | source)
XLA Modules:
  0.0 173.7 jit_solution(13296419147776490798)
XLA Ops:
  2.0 9.6 %collective-permute-done = bf16[48,254]{1,0:T(8,128)(2,1)S(1)} collective-permute-done((bf16[48,254]{1,0:T(8,128)(2,1)S(1)}, bf16[48,254]{1,0:T(8,128)(2,1)S(1)}, u32[]{:S(2)}, u32[]{:S(2)}) %collective-permute-start) | collective-permute-done | bytes 24416 | tf_op jit(solution)/shard_map/ppermute | solution.py:14
  13.9 8.9 %all-to-all-start = ((bf16[32,48,766]{2,1,0:T(8,128)(2,1)}), bf16[32,48,766]{2,1,0:T(8,128)(2,1)S(1)}, u32[]{:S(2)}, u32[]{:S(2)}) async-start(bf16[32,48,766]{2,1,0:T(8,128)(2,1)} %stack.8), calls=%async_computation | async-start | bytes 4718592 | tf_op jit(solution)/shard_map/all_to_all | solution.py:64
  23.4 5.0 %sine_convert_fusion = (bf16[766,384]{1,0:T(8,128)(2,1)S(1)}, bf16[766,384]{1,0:T(8,128)(2,1)S(1)}) fusion(), kind=kLoop, calls=%fused_computation.41 | loop fusion | flops 3235584 | bytes 1176576 | tf_op jit(solution)/shard_map/convert.1
  29.4 4.2 %fusion.30 = (f32[512,384]{1,0:T(8,128)S(1)}, f32[512,384]{1,0:T(8,128)}) fusion(), kind=kLoop, calls=%fused_computation.54 | loop fusion | flops 1769472 | bytes 1572864 | tf_op jit(solution)/shard_map/sin | solution.py:21
  33.8 3.0 %convolution_bitcast_fusion = f32[1536,768]{0,1:T(8,128)} fusion(bf16[200,768]{1,0:T(8,128)(2,1)S(1)} %pad_maximum_fusion.7, bf16[1536,200]{1,0:T(8,128)(2,1)S(1)} %bitcast.25), kind=kOutput, calls=%fused_computation.2 | convolution fusion | flops 471859200 | bytes 5640192 | tf_op jit(solution)/shard_map/dot_general | solution.py:26
  36.8 3.0 %convolution_bitcast_fusion.1 = f32[1536,768]{0,1:T(8,128)} fusion(bf16[200,768]{1,0:T(8,128)(2,1)S(1)} %pad_maximum_fusion.7, bf16[1536,200]{1,0:T(8,128)(2,1)S(1)} %bitcast.24), kind=kOutput, calls=%fused_computation.3 | convolution fusion | flops 471859200 | bytes 5640192 | tf_op jit(solution)/shard_map/dot_general | solution.py:26
  39.7 38.4 %all-to-all-done = bf16[32,48,766]{2,1,0:T(8,128)(2,1)S(1)} async-done(((bf16[32,48,766]{2,1,0:T(8,128)(2,1)}), bf16[32,48,766]{2,1,0:T(8,128)(2,1)S(1)}, u32[]{:S(2)}, u32[]{:S(2)}) %all-to-all-start) | async-done | bytes 2353184 | tf_op jit(solution)/shard_map/all_to_all | solution.py:64
  79.5 4.0 %convolution_convert_fusion = bf16[1536,768]{1,0:T(8,128)(2,1)S(1)} fusion(bf16[1536,766]{1,0:T(8,128)(2,1)} %bitcast.26, bf16[766,384]{1,0:T(8,128)(2,1)} %copy-done.4, bf16[766,384]{1,0:T(8,128)(2,1)} %copy-done.5), kind=kOutput, calls=%fused_computation.6 | convolution fusion | flops 1810753536 | bytes 5889024 | tf_op jit(solution)/shard_map/dot_general | solution.py:62
  83.5 5.7 %gather_fusion.1 = bf16[1536,768]{1,0:T(8,128)(2,1)} fusion(bf16[1536,768]{1,0:T(8,128)(2,1)S(1)} %convolution_convert_fusion, s32[2048]{0:T(1024)S(1)} %pad_clamp_fusion), kind=kCustom, calls=%fused_computation.1 | custom fusion | bytes 4724736 | tf_op jit(solution)/shard_map/gather | solution.py:39
  89.1 4.3 %copy.10 = bf16[1536,768]{0,1:T(8,128)(2,1)} copy(bf16[1536,768]{1,0:T(8,128)(2,1)} %gather_fusion.1) | data formatting | bytes 4718592 | tf_op jit(solution)/shard_map/gather | solution.py:39
  93.4 2.3 %convert_element_type.31 = f32[1536,768]{0,1:T(8,128)S(1)} convert(bf16[1536,768]{0,1:T(8,128)(2,1)} %copy.10) | non-fusion elementwise | flops 1179648 | bytes 7077888 | tf_op jit(solution)/shard_map/convert_element_type | solution.py:39
  95.7 13.5 %multiply_subtract_fusion = (f32[1536,384]{0,1:T(8,128)}, f32[1536,384]{0,1:T(8,128)S(1)}, f32[1536,384]{0,1:T(8,128)S(1)}) fusion(s32[1536]{0:T(1024)S(1)} %mul.198, f32[1536,768]{0,1:T(8,128)S(1)} %convert_element_type.31, f32[1536,768]{0,1:T(8,128)} %convolution_bitcast_fusion), kind=kLoop, calls=%fused_computation.12 | loop fusion | flops 10616832 | bytes 16521216 | tf_op jit(solution)/shard_map/sub | solution.py:43
  109.3 10.8 %multiply_add_fusion = f32[1536,384]{0,1:T(8,128)} fusion(f32[1536,384]{0,1:T(8,128)S(1)} %get-tuple-element.10, f32[1536,384]{0,1:T(8,128)S(1)} %get-tuple-element.9, s32[1536]{0:T(1024)S(1)} %mul.198), kind=kLoop, calls=%fused_computation.11 | loop fusion | flops 7077888 | bytes 7084032 | tf_op jit(solution)/shard_map/add | solution.py:44
  120.0 3.1 %copy.12 = f32[1536,384]{1,0:T(8,128)} copy(f32[1536,384]{0,1:T(8,128)} %multiply_add_fusion) | data formatting | bytes 4718592 | tf_op jit(solution)/shard_map/add | solution.py:44
  123.2 5.7 %gather_fusion = bf16[1536,768]{1,0:T(8,128)(2,1)} fusion(bf16[1536,768]{1,0:T(8,128)(2,1)S(1)} %convolution_convert_fusion, s32[2048]{0:T(1024)S(1)} %pad_clamp_fusion.1), kind=kCustom, calls=%fused_computation | custom fusion | bytes 4724736 | tf_op jit(solution)/shard_map/gather | solution.py:39
  128.9 2.8 %copy.7 = bf16[1536,768]{0,1:T(8,128)(2,1)S(1)} copy(bf16[1536,768]{1,0:T(8,128)(2,1)} %gather_fusion) | data formatting | bytes 4718592 | tf_op jit(solution)/shard_map/gather | solution.py:39
  132.3 13.5 %multiply_subtract_fusion.2 = (f32[1536,384]{0,1:T(8,128)}, f32[1536,384]{0,1:T(8,128)S(1)}, f32[1536,384]{0,1:T(8,128)S(1)}) fusion(s32[1536]{0:T(1024)S(1)} %mul.177, f32[1536,768]{0,1:T(8,128)S(1)} %convert_element_type.28, f32[1536,768]{0,1:T(8,128)} %convolution_bitcast_fusion.1), kind=kLoop, calls=%fused_computation.21 | loop fusion | flops 10616832 | bytes 16521216 | tf_op jit(solution)/shard_map/sub | solution.py:43
  145.9 9.9 %multiply_add_fusion.2 = f32[1536,384]{0,1:T(8,128)S(1)} fusion(f32[1536,384]{0,1:T(8,128)S(1)} %get-tuple-element.7, f32[1536,384]{0,1:T(8,128)S(1)} %get-tuple-element.6, s32[1536]{0:T(1024)S(1)} %mul.177), kind=kLoop, calls=%fused_computation.20 | loop fusion | flops 7077888 | bytes 7084032 | tf_op jit(solution)/shard_map/add | solution.py:44
  155.7 2.0 %copy.9 = f32[1536,384]{1,0:T(8,128)} copy(f32[1536,384]{0,1:T(8,128)S(1)} %multiply_add_fusion.2) | data formatting | bytes 4718592 | tf_op jit(solution)/shard_map/add | solution.py:44
  157.7 2.0 %reduce_sum.39 = f32[32,384]{1,0:T(8,128)S(1)} reduce(f32[32,48,384]{2,1,0:T(8,128)} %bitcast.20, f32[]{:T(128)} %constant.26.clone.1), dimensions={1}, to_apply=%region_3.4 | reduce | flops 577536 | bytes 2408452 | tf_op jit(solution)/shard_map/reduce_sum | solution.py:44
  161.6 2.0 %copy.11 = f32[1536,384]{1,0:T(8,128)} copy(f32[1536,384]{0,1:T(8,128)S(1)} %copy-done) | data formatting | bytes 4718592 | tf_op jit(solution)/shard_map/sub | solution.py:43
  163.6 2.0 %reduce_sum.38 = f32[32,384]{1,0:T(8,128)S(1)} reduce(f32[32,48,384]{2,1,0:T(8,128)} %bitcast.23, f32[]{:T(128)} %constant.26.clone.1), dimensions={1}, to_apply=%region_2.3 | reduce | flops 577536 | bytes 2408452 | tf_op jit(solution)/shard_map/reduce_sum | solution.py:43
  166.0 2.0 %copy.8 = f32[1536,384]{1,0:T(8,128)} copy(f32[1536,384]{0,1:T(8,128)S(1)} %copy-done.1) | data formatting | bytes 4718592 | tf_op jit(solution)/shard_map/sub | solution.py:43
  168.0 1.9 %reduce_sum.36 = f32[32,384]{1,0:T(8,128)S(1)} reduce(f32[32,48,384]{2,1,0:T(8,128)} %bitcast.22, f32[]{:T(128)} %constant.26.clone.1), dimensions={1}, to_apply=%region_0.1 | reduce | flops 577536 | bytes 2408452 | tf_op jit(solution)/shard_map/reduce_sum | solution.py:43
  (41 shorter events, 13.9 us)
Async XLA Ops:
  0.7 10.8 %collective-permute-start = (bf16[48,254]{1,0:T(8,128)(2,1)S(1)}, bf16[48,254]{1,0:T(8,128)(2,1)S(1)}, u32[]{:S(2)}, u32[]{:S(2)}) collective-permute-start(bf16[48,254]{1,0:T(8,128)(2,1)S(1)} %slice.52), channel_id=1, source_target_pairs={{1,0},{2,1},{3,2},{4,3},{5,4},{6,5},{7,6},{9,8},{10,9},{11,10},{12... | collective-permute-start | bytes 73160 | tf_op jit(solution)/shard_map/ppermute | solution.py:14
  13.9 8.9 %copy-start.7 = (s32[2,32,48]{2,1,0:T(8,128)S(1)}, s32[2,32,48]{2,1,0:T(8,128)}, u32[]{:S(2)}) copy-start(s32[2,32,48]{2,1,0:T(8,128)} %param.6) | copy-start | bytes 36868
  13.9 9.0 %copy-start.8 = (s32[2,32,48]{2,1,0:T(8,128)S(1)}, s32[2,32,48]{2,1,0:T(8,128)}, u32[]{:S(2)}) copy-start(s32[2,32,48]{2,1,0:T(8,128)} %param.7) | copy-start | bytes 36868
  13.9 64.2 %all-to-all-start = ((bf16[32,48,766]{2,1,0:T(8,128)(2,1)}), bf16[32,48,766]{2,1,0:T(8,128)(2,1)S(1)}, u32[]{:S(2)}, u32[]{:S(2)}) async-start(bf16[32,48,766]{2,1,0:T(8,128)(2,1)} %stack.8), calls=%async_computation | async-start | bytes 4718592 | tf_op jit(solution)/shard_map/all_to_all | solution.py:64
  23.2 10.4 %copy-start.6 = (bf16[2,32,48,200]{3,2,1,0:T(8,128)(2,1)S(1)}, bf16[2,32,48,200]{3,2,1,0:T(8,128)(2,1)}, u32[]{:S(2)}) copy-start(bf16[2,32,48,200]{3,2,1,0:T(8,128)(2,1)} %param.5) | copy-start | bytes 3686404
  28.4 0.8 copy-start.4
  28.4 1.0 copy-start.5
  78.1 1.4 copy-start.3
  157.7 3.9 %copy-start = (f32[1536,384]{0,1:T(8,128)S(1)}, f32[1536,384]{0,1:T(8,128)}, u32[]{:S(2)}) copy-start(f32[1536,384]{0,1:T(8,128)} %get-tuple-element.8) | copy-start | bytes 7077892
  163.6 2.4 %copy-start.1 = (f32[1536,384]{0,1:T(8,128)S(1)}, f32[1536,384]{0,1:T(8,128)}, u32[]{:S(2)}) copy-start(f32[1536,384]{0,1:T(8,128)} %get-tuple-element.5) | copy-start | bytes 7077892
  168.0 2.0 %copy-start.2 = (f32[512,384]{1,0:T(8,128)S(1)}, f32[512,384]{1,0:T(8,128)}, u32[]{:S(2)}) copy-start(f32[512,384]{1,0:T(8,128)} %get-tuple-element.24) | copy-start | bytes 2359300
